TPU v7x, 512 devices: a whole 4x4x16 slice. The times are simulated.
512 devices in a mesh: expert: 128 (over y, x_lo, z), half: 4 (over x_hi, core).
Axes of the slice: x: 4 (x_hi: 2, x_lo: 2; x = x_hi * 2 + x_lo), y: 4, z: 16, core: 2. Of those that a mesh axis runs over, the one named last changes fastest.
Arguments:
- tokens: bfloat16 [25088, 1024], P('expert', 'half'), may hold values from -128 to 128
- slot_params: bfloat16 [1024, 256], P('half'), may hold values from -0.5 to 0.5
- w_up: bfloat16 [128, 1024, 4096], P('expert', None, 'half'), may hold values from -0.1875 to 0.1875
- w_down: bfloat16 [128, 4096, 1024], P('expert', 'half'), may hold values from -0.09375 to 0.09375
- cotangent: bfloat16 [25088, 1024], P('expert', 'half'), may hold values from -6 to 6
Outputs:
- mixed: bfloat16 [25088, 1024], P('expert', 'half')
- grad_tokens: bfloat16 [25088, 1024], P('expert', 'half')
- grad_params: float32 [1024, 256], P('half')
All inputs are finite; a program needn't handle non-finite values.
Results may differ from a plain program's by a relative error of at most 0.017.
Values may be sent and summed in bfloat16 or wider, within the bound.
A program may use at most 64 MiB of HBM per device.

v0:
```python
import jax
import jax.numpy as jnp
from jax import lax
from jax.sharding import PartitionSpec as P

SEQ = 196
SLOTS = 2
EXPERT = ("y", "x_lo", "z")
HALF = ("x_hi", "core")


def gelu_grad(preact, upstream):
    pullback = jax.vjp(jax.nn.gelu, preact)[1]
    return pullback(upstream)[0]


def softmax_back(probabilities, upstream, over_axis):
    inner = jnp.sum(probabilities * upstream, axis=over_axis, keepdims=True)
    return probabilities * (upstream - inner)


def local(tokens, slot_params, w_up, w_down, cotangent):
    feat_quarter = tokens.shape[1]
    images = tokens.shape[0] // SEQ
    columns = slot_params.shape[1]
    experts = columns // SLOTS
    up_matrix = w_up[0]
    down_matrix = w_down[0]
    inputs = tokens.reshape(images, SEQ, feat_quarter)
    upstream = cotangent.reshape(images, SEQ, feat_quarter)
    partial_logits = jnp.einsum(
        "imf,fc->imc", inputs, slot_params, preferred_element_type=jnp.float32
    )
    logits = lax.psum(partial_logits, HALF)
    dispatch = jax.nn.softmax(logits, axis=1)
    combine = jax.nn.softmax(logits, axis=2)
    dispatch_bf = dispatch.astype(jnp.bfloat16).reshape(images, SEQ, experts, SLOTS)
    combine_bf = combine.astype(jnp.bfloat16).reshape(images, SEQ, experts, SLOTS)
    slot_in = jnp.einsum(
        "imes,imf->sife", dispatch_bf, inputs, preferred_element_type=jnp.float32
    ).astype(jnp.bfloat16)
    received = lax.all_to_all(slot_in, EXPERT, split_axis=3, concat_axis=3, tiled=True)
    up_slice = up_matrix
    preact = jnp.einsum(
        "sifr,fk->sirk",
        lax.all_gather(received, HALF, axis=2, tiled=True),
        up_slice,
        preferred_element_type=jnp.float32,
    )
    hidden = jax.nn.gelu(preact).astype(jnp.bfloat16)
    down_slice = down_matrix
    summed = lax.psum(
        jnp.einsum("kf,sirk->fsir", down_slice, hidden, preferred_element_type=jnp.float32).astype(
            jnp.bfloat16
        ),
        HALF,
    ).astype(jnp.float32)
    slot_out = lax.dynamic_slice_in_dim(
        summed, lax.axis_index(HALF) * feat_quarter, feat_quarter, 0
    )
    returned = lax.all_to_all(
        slot_out.astype(jnp.bfloat16), EXPERT, split_axis=3, concat_axis=3, tiled=True
    )
    mixed = jnp.einsum(
        "imes,fsie->imf", combine_bf, returned, preferred_element_type=jnp.float32
    ).astype(jnp.bfloat16)
    grad_slot_out = jnp.einsum(
        "imes,imf->sife", combine_bf, upstream, preferred_element_type=jnp.float32
    ).astype(jnp.bfloat16)
    combine_part = jnp.einsum(
        "imf,fsie->imes", upstream, returned, preferred_element_type=jnp.float32
    ).reshape(images, SEQ, columns)
    grad_combine = lax.psum(combine_part.astype(jnp.bfloat16), HALF).astype(jnp.float32)
    grad_received = lax.all_to_all(grad_slot_out, EXPERT, split_axis=3, concat_axis=3, tiled=True)
    down_slice = down_matrix
    grad_hidden = jnp.einsum(
        "sifr,kf->sirk",
        lax.all_gather(grad_received, HALF, axis=2, tiled=True),
        down_slice,
        preferred_element_type=jnp.float32,
    )
    grad_preact = gelu_grad(preact, grad_hidden).astype(jnp.bfloat16)
    up_slice = up_matrix
    summed_grad = lax.psum(
        jnp.einsum(
            "fk,sirk->fsir", up_slice, grad_preact, preferred_element_type=jnp.float32
        ).astype(jnp.bfloat16),
        HALF,
    ).astype(jnp.float32)
    grad_slot_in = lax.dynamic_slice_in_dim(
        summed_grad, lax.axis_index(HALF) * feat_quarter, feat_quarter, 0
    )
    grad_returned = lax.all_to_all(
        grad_slot_in.astype(jnp.bfloat16), EXPERT, split_axis=3, concat_axis=3, tiled=True
    )
    dispatch_part = jnp.einsum(
        "imf,fsie->imes", inputs, grad_returned, preferred_element_type=jnp.float32
    ).reshape(images, SEQ, columns)
    grad_dispatch = lax.psum(dispatch_part.astype(jnp.bfloat16), HALF).astype(jnp.float32)
    grad_logits = softmax_back(combine, grad_combine, 2) + softmax_back(dispatch, grad_dispatch, 1)
    grad_logit_bf = grad_logits.astype(jnp.bfloat16)
    token_term = jnp.einsum(
        "imes,fsie->imf", dispatch_bf, grad_returned, preferred_element_type=jnp.float32
    )
    logit_term = jnp.einsum(
        "imc,fc->imf", grad_logit_bf, slot_params, preferred_element_type=jnp.float32
    )
    grad_tokens = (token_term + logit_term).astype(jnp.bfloat16).reshape(images * SEQ, feat_quarter)
    params_part = jnp.einsum(
        "imf,imc->fc", inputs, grad_logit_bf, preferred_element_type=jnp.float32
    )
    grad_params = lax.psum(lax.psum(lax.psum(params_part, "z"), "y"), "x_lo")
    return (mixed.reshape(images * SEQ, feat_quarter), grad_tokens, grad_params)


def solution(mesh):
    mesh = jax.sharding.Mesh(mesh.devices.reshape(4, 2, 16, 2, 2), EXPERT + HALF)
    in_specs = (
        P(EXPERT, HALF),
        P(HALF, None),
        P(EXPERT, None, HALF),
        P(EXPERT, HALF, None),
        P(EXPERT, HALF),
    )
    out_specs = (P(EXPERT, HALF), P(EXPERT, HALF), P(HALF, None))
    return jax.shard_map(local, mesh=mesh, in_specs=in_specs, out_specs=out_specs, check_vma=False)
```

profile of v0, /device:TPU:1, one launch (start us, length us, event | category | flops | bytes accessed | tf_op | source)
XLA Modules:
  0.0 566.3 jit_solution(11431547479652277655)
XLA Ops:
  7.2 2.0 convolution_bitcast_fusion.3
  9.2 64.2 %all-reduce.9.cloned.1.call-done = f32[1,196,256]{2,1,0:T(8,128)} async-done(((f32[1,196,256]{2,1,0:T(8,128)}), f32[1,196,256]{2,1,0:T(8,128)}) %all-reduce.9.cloned.1.call-update) | async-done | bytes 200720 | tf_op jit(solution)/shard_map/psum | solution.py:34
  73.4 1.0 fusion.82
  74.5 1.1 fusion.60
  75.6 1.1 fusion.80
  78.1 16.6 %all-to-all-start = ((bf16[2,1,256,128]{2,0,1,3:T(2,128)(2,1)}), bf16[2,1,256,128]{2,0,1,3:T(2,128)(2,1)S(1)}, u32[]{:S(2)}, u32[]{:S(2)}) async-start(bf16[2,1,256,128]{2,0,1,3:T(2,128)(2,1)} %copy.37), calls=%async_computation | async-start | bytes 262144 | tf_op jit(solution)/shard_map/all_to_all | solution.py:42
  96.1 15.3 %all-to-all-done = bf16[2,1,256,128]{2,0,1,3:T(2,128)(2,1)S(1)} async-done(((bf16[2,1,256,128]{2,0,1,3:T(2,128)(2,1)}), bf16[2,1,256,128]{2,0,1,3:T(2,128)(2,1)S(1)}, u32[]{:S(2)}, u32[]{:S(2)}) %all-to-all-start) | async-done | bytes 131104 | tf_op jit(solution)/shard_map/all_to_all | solution.py:42
  111.4 6.6 %all-to-all-start.2 = ((bf16[2,1,256,128]{2,0,1,3:T(2,128)(2,1)}), bf16[2,1,256,128]{2,0,1,3:T(2,128)(2,1)S(1)}, u32[]{:S(2)}, u32[]{:S(2)}) async-start(bf16[2,1,256,128]{2,0,1,3:T(2,128)(2,1)} %copy.43), calls=%async_computation.2 | async-start | bytes 262144 | tf_op jit(solution)/shard_map/all_to_all | solution.py:74
  118.1 10.0 %all_gather.6 = bf16[2,1,1024,128]{2,3,0,1:T(8,128)(2,1)S(1)} all-gather(bf16[2,1,256,128]{2,3,0,1:T(8,128)(2,1)S(1)} %copy.38), channel_id=1, replica_groups=mesh['y'=4,'x_lo'=2,'z'=16,'x_hi'=2,'core'=2] {'x_hi','core'}, dimensions={2}, use_global_device_ids=true | all-gather | bytes 655360 | tf_op jit(solution)/shard_map/all_gather | solution.py:46
  128.1 5.5 all-to-all-done.2
  133.6 11.5 %all_gather.7 = bf16[2,1,1024,128]{2,3,0,1:T(8,128)(2,1)S(1)} all-gather(bf16[2,1,256,128]{2,3,0,1:T(8,128)(2,1)S(1)} %copy.44), channel_id=1, replica_groups=mesh['y'=4,'x_lo'=2,'z'=16,'x_hi'=2,'core'=2] {'x_hi','core'}, dimensions={2}, use_global_device_ids=true | all-gather | bytes 655360 | tf_op jit(solution)/shard_map/all_gather | solution.py:78
  145.1 2.3 fusion.6
  147.4 1.0 copy-done.3
  148.4 1.6 fusion.14
  150.0 4.5 fusion.17
  154.5 52.4 %all-reduce.19.cloned.1.call-done = (bf16[1024,2,1,128]{0,3,1,2:T(8,128)(2,1)}, bf16[1024,2,1,128]{0,3,1,2:T(8,128)(2,1)}) async-done(((bf16[1024,2,1,128]{0,3,1,2:T(8,128)(2,1)}, bf16[1024,2,1,128]{0,3,1,2:T(8,128)(2,1)}), (bf16[1024,2,1,128]{0,3,1,2:T(8,128)(2,1)}, bf16[1024,2,1,128]{0,3,1,2:T(8,128)(2,1)})) %all-reduce.19.cloned.1.call-update) | async-done | bytes 1048592 | tf_op jit(solution)/shard_map/psum | solution.py:52
  207.0 0.9 convert_convert_fusion
  208.7 16.6 %all-to-all-start.3 = ((bf16[256,2,1,128]{0,1,2,3:T(2,128)(2,1)}), bf16[256,2,1,128]{0,1,2,3:T(2,128)(2,1)S(1)}, u32[]{:S(2)}, u32[]{:S(2)}) async-start(bf16[256,2,1,128]{0,1,2,3:T(2,128)(2,1)} %copy.45), calls=%async_computation.3 | async-start | bytes 262144 | tf_op jit(solution)/shard_map/all_to_all | solution.py:93
  225.3 0.9 convert_convert_fusion.1
  227.0 15.0 %all-to-all-done.3 = bf16[256,2,1,128]{0,1,2,3:T(2,128)(2,1)S(1)} async-done(((bf16[256,2,1,128]{0,1,2,3:T(2,128)(2,1)}), bf16[256,2,1,128]{0,1,2,3:T(2,128)(2,1)S(1)}, u32[]{:S(2)}, u32[]{:S(2)}) %all-to-all-start.3) | async-done | bytes 131104 | tf_op jit(solution)/shard_map/all_to_all | solution.py:93
  242.0 6.8 %all-to-all-start.1 = ((bf16[256,2,1,128]{0,1,2,3:T(2,128)(2,1)}), bf16[256,2,1,128]{0,1,2,3:T(2,128)(2,1)S(1)}, u32[]{:S(2)}, u32[]{:S(2)}) async-start(bf16[256,2,1,128]{0,1,2,3:T(2,128)(2,1)} %copy.39), calls=%async_computation.1 | async-start | bytes 262144 | tf_op jit(solution)/shard_map/all_to_all | solution.py:61
  250.3 14.1 %all-to-all-done.1 = bf16[256,2,1,128]{0,1,2,3:T(2,128)(2,1)S(1)} async-done(((bf16[256,2,1,128]{0,1,2,3:T(2,128)(2,1)}), bf16[256,2,1,128]{0,1,2,3:T(2,128)(2,1)S(1)}, u32[]{:S(2)}, u32[]{:S(2)}) %all-to-all-start.1) | async-done | bytes 131104 | tf_op jit(solution)/shard_map/all_to_all | solution.py:61
  265.8 48.2 %all-reduce.17.cloned.1.call-done = (bf16[1,196,256]{2,1,0:T(8,128)(2,1)}, bf16[1,196,256]{2,1,0:T(8,128)(2,1)}) async-done(((bf16[1,196,256]{2,1,0:T(8,128)(2,1)}, bf16[1,196,256]{2,1,0:T(8,128)(2,1)}), (bf16[1,196,256]{2,1,0:T(8,128)(2,1)}, bf16[1,196,256]{2,1,0:T(8,128)(2,1)})) %all-reduce.17.cloned.1.call-update) | async-done | bytes 200720 | tf_op jit(solution)/shard_map/psum | solution.py:99
  314.0 1.2 fusion.51
  315.2 1.1 fusion.65
  316.3 0.9 convolution_bitcast_fusion
  317.3 126.5 %all-reduce.11.cloned.1.call-done = f32[256,256]{0,1:T(8,128)} async-done(((f32[256,256]{0,1:T(8,128)}), f32[256,256]{0,1:T(8,128)}) %all-reduce.11.cloned.1.call-update) | async-done | bytes 262160 | tf_op jit(solution)/shard_map/psum | solution.py:112
  443.9 0.9 fusion.20
  444.8 62.7 %all-reduce.13.cloned.1.call-done = f32[256,256]{0,1:T(8,128)} async-done(((f32[256,256]{0,1:T(8,128)}), f32[256,256]{0,1:T(8,128)}) %all-reduce.13.cloned.1.call-update) | async-done | bytes 262160 | tf_op jit(solution)/shard_map/psum | solution.py:112
  507.7 0.9 fusion.21
  508.6 49.1 %all-reduce.15.cloned.1.call-done = f32[256,256]{0,1:T(8,128)} async-done(((f32[256,256]{0,1:T(8,128)}), f32[256,256]{0,1:T(8,128)}) %all-reduce.15.cloned.1.call-update) | async-done | bytes 262160 | tf_op jit(solution)/shard_map/psum | solution.py:112
  557.6 1.8 copy.52
  (66 shorter events, 7.6 us)
Async XLA Ops:
  7.2 141.2 %copy-start = (bf16[1,1024,1024]{2,1,0:T(8,128)(2,1)S(1)}, bf16[1,1024,1024]{2,1,0:T(8,128)(2,1)}, u32[]{:S(2)}) copy-start(bf16[1,1024,1024]{2,1,0:T(8,128)(2,1)} %param.8) | copy-start | bytes 6291460
  7.2 69.9 %copy-start.2 = (bf16[196,256]{1,0:T(8,128)(2,1)S(1)}, bf16[196,256]{1,0:T(8,128)(2,1)}, u32[]{:S(2)}) copy-start(bf16[196,256]{1,0:T(8,128)(2,1)} %param.5) | copy-start | bytes 301060
  7.2 87.9 %copy-start.5 = (bf16[196,256]{1,0:T(8,128)(2,1)S(1)}, bf16[196,256]{1,0:T(8,128)(2,1)}, u32[]{:S(2)}) copy-start(bf16[196,256]{1,0:T(8,128)(2,1)} %param.9) | copy-start | bytes 301060
  7.2 66.2 %all-reduce.9.cloned.1.call-start = ((), (), s32[]{:S(2)}) async-start(), calls=%async_computation.4 | async-start | bytes 409600 | tf_op jit(solution)/shard_map/psum | solution.py:34
  74.5 2.2 copy-start.7
  74.5 2.2 copy-start.9
  75.6 1.1 copy-start.11
  75.6 1.1 copy-start.13
  78.1 33.3 %all-to-all-start = ((bf16[2,1,256,128]{2,0,1,3:T(2,128)(2,1)}), bf16[2,1,256,128]{2,0,1,3:T(2,128)(2,1)S(1)}, u32[]{:S(2)}, u32[]{:S(2)}) async-start(bf16[2,1,256,128]{2,0,1,3:T(2,128)(2,1)} %copy.37), calls=%async_computation | async-start | bytes 262144 | tf_op jit(solution)/shard_map/all_to_all | solution.py:42
  111.4 22.2 %all-to-all-start.2 = ((bf16[2,1,256,128]{2,0,1,3:T(2,128)(2,1)}), bf16[2,1,256,128]{2,0,1,3:T(2,128)(2,1)S(1)}, u32[]{:S(2)}, u32[]{:S(2)}) async-start(bf16[2,1,256,128]{2,0,1,3:T(2,128)(2,1)} %copy.43), calls=%async_computation.2 | async-start | bytes 262144 | tf_op jit(solution)/shard_map/all_to_all | solution.py:74
  118.1 88.9 %all-reduce.19.cloned.1.call-start = ((), (), s32[]{:S(2)}) async-start(), calls=%async_computation.9 | async-start | bytes 2097152 | tf_op jit(solution)/shard_map/psum | solution.py:52
  147.4 1.0 copy-start.3
  154.5 110.0 %copy-start.6 = (bf16[196,256]{1,0:T(8,128)(2,1)S(1)}, bf16[196,256]{1,0:T(8,128)(2,1)}, u32[]{:S(2)}) copy-start(bf16[196,256]{1,0:T(8,128)(2,1)} %param.9) | copy-start | bytes 301060
  207.9 106.2 %copy-start.1 = (f32[1,196,256]{2,1,0:T(8,128)S(1)}, f32[1,196,256]{2,1,0:T(8,128)}, u32[]{:S(2)}) copy-start(f32[1,196,256]{2,1,0:T(8,128)} %all-reduce.9.cloned.1.call-done) | copy-start | bytes 602116
  207.9 106.1 %copy-start.8 = (f32[256]{0:T(256)S(1)}, f32[256]{0:T(256)}, u32[]{:S(2)}) copy-start(f32[256]{0:T(256)} %copy-done.7) | copy-start | bytes 3076
  207.9 106.1 %copy-start.10 = (f32[196]{0:T(256)S(1)}, f32[196]{0:T(256)}, u32[]{:S(2)}) copy-start(f32[196]{0:T(256)} %copy-done.9) | copy-start | bytes 2356
  207.9 106.1 %copy-start.12 = (f32[256]{0:T(256)S(1)}, f32[256]{0:T(256)}, u32[]{:S(2)}) copy-start(f32[256]{0:T(256)} %copy-done.11) | copy-start | bytes 3076
  207.9 106.1 %copy-start.14 = (f32[196]{0:T(256)S(1)}, f32[196]{0:T(256)}, u32[]{:S(2)}) copy-start(f32[196]{0:T(256)} %copy-done.13) | copy-start | bytes 2356
  208.7 33.3 %all-to-all-start.3 = ((bf16[256,2,1,128]{0,1,2,3:T(2,128)(2,1)}), bf16[256,2,1,128]{0,1,2,3:T(2,128)(2,1)S(1)}, u32[]{:S(2)}, u32[]{:S(2)}) async-start(bf16[256,2,1,128]{0,1,2,3:T(2,128)(2,1)} %copy.45), calls=%async_computation.3 | async-start | bytes 262144 | tf_op jit(solution)/shard_map/all_to_all | solution.py:93
  242.0 22.3 %all-to-all-start.1 = ((bf16[256,2,1,128]{0,1,2,3:T(2,128)(2,1)}), bf16[256,2,1,128]{0,1,2,3:T(2,128)(2,1)S(1)}, u32[]{:S(2)}, u32[]{:S(2)}) async-start(bf16[256,2,1,128]{0,1,2,3:T(2,128)(2,1)} %copy.39), calls=%async_computation.1 | async-start | bytes 262144 | tf_op jit(solution)/shard_map/all_to_all | solution.py:61
  248.8 65.2 %all-reduce.17.cloned.1.call-start = ((), (), s32[]{:S(2)}) async-start(), calls=%async_computation.8 | async-start | bytes 409600 | tf_op jit(solution)/shard_map/psum | solution.py:99
  264.5 243.2 %copy-start.4 = (bf16[256,256]{1,0:T(8,128)(2,1)S(1)}, bf16[256,256]{1,0:T(8,128)(2,1)}, u32[]{:S(2)}) copy-start(bf16[256,256]{1,0:T(8,128)(2,1)} %param.6) | copy-start | bytes 393220
  265.8 178.0 %all-reduce.11.cloned.1.call-start = ((), (), s32[]{:S(2)}) async-start(), calls=%async_computation.5 | async-start | bytes 524288 | tf_op jit(solution)/shard_map/psum | solution.py:112
  317.3 190.1 %all-reduce.13.cloned.1.call-start = ((), (), s32[]{:S(2)}) async-start(), calls=%async_computation.6 | async-start | bytes 524288 | tf_op jit(solution)/shard_map/psum | solution.py:112
  443.9 113.8 %all-reduce.15.cloned.1.call-start = ((), (), s32[]{:S(2)}) async-start(), calls=%async_computation.7 | async-start | bytes 524288 | tf_op jit(solution)/shard_map/psum | solution.py:112
Sparse Core Ops, SparseCore 0:
  11.5 61.8 all-reduce.8
  154.7 52.2 all-reduce.18
  265.9 48.0 all-reduce.16
  317.4 126.3 all-reduce.10
  446.0 61.3 all-reduce.12
  510.2 47.4 all-reduce.14
where the time goes:
time: 567 us; the launch traced here: 566 us
  waiting for transfers between devices  453 us (80%)
  starting transfers between devices  46.9 us (8%)
  blocking collectives  21.4 us (4%)
  between operations  14.5 us (3%)
  matrix products  14.1 us (2%)
  local copies, waits for them, and re-layouts  8.99 us (2%)
  other arithmetic  7.34 us (1%)
    psum x3, waiting for transfers between devices, local(): grad_params = lax.psum(lax.psum(lax.psum(params_part, 'z'), 'y'), 'x_lo')  238 us
    psum x1, waiting for transfers between devices, local(): logits = lax.psum(partial_logits, HALF)  64.2 us
    psum x1, waiting for transfers between devices, local(): lax.psum(jnp.einsum('kf,sirk->fsir', down_slice, hidden, preferred_elemen...  52.4 us
    psum x1, waiting for transfers between devices, local(): lax.psum(dispatch_part.astype(jnp.bfloat16), HALF).astype(jnp.float32)  48.2 us
    all_to_all x1, starting transfers between devices, local(): lax.all_to_all(grad_slot_in.astype(jnp.bfloat16), EXPERT, split_axis=3, c...  16.6 us
    all_to_all x1, starting transfers between devices, local(): lax.all_to_all(slot_in, EXPERT, split_axis=3, concat_axis=3, tiled=True)  16.6 us
    all_to_all x1, waiting for transfers between devices, local(): lax.all_to_all(slot_in, EXPERT, split_axis=3, concat_axis=3, tiled=True)  15.3 us
    all_to_all x1, waiting for transfers between devices, local(): lax.all_to_all(grad_slot_in.astype(jnp.bfloat16), EXPERT, split_axis=3, c...  15 us
  transfers between devices with their start and end apart: 10, of which 10 were waited for; matrix products, arithmetic and copies ran while one was open for 1% of the time, Pallas kernels for 0%

commit v1 on v0

--- a/solution.py
+++ b/solution.py
@@ -31,7 +31,7 @@
     partial_logits = jnp.einsum(
         "imf,fc->imc", inputs, slot_params, preferred_element_type=jnp.float32
     )
-    logits = lax.psum(partial_logits, HALF)
+    logits = jnp.sum(lax.all_gather(partial_logits, axis_name=HALF), 0)
     dispatch = jax.nn.softmax(logits, axis=1)
     combine = jax.nn.softmax(logits, axis=2)
     dispatch_bf = dispatch.astype(jnp.bfloat16).reshape(images, SEQ, experts, SLOTS)

time: 567 us -> 515 us (0.908)
  waiting for transfers between devices: 453 us -> 388 us
  blocking collectives: 21.4 us -> 38.5 us
    psum x1 -> x0, waiting for transfers between devices: 64.2 us -> none  [local(): logits = lax.psum(partial_logits, HALF)]
    all_gather x0 -> x1, blocking collectives: none -> 15.6 us  [local(): logits = jnp.sum(lax.all_gather(partial_logits, axis_name=HALF), 0)]
  transfers between devices with their start and end apart: 10 -> 9, of which waited for: 10 -> 9; matrix products, arithmetic and copies ran while one was open for 1% -> 1% of each run, Pallas kernels for 0% -> 0%
where the time goes in v1:
time: 515 us
  waiting for transfers between devices  388 us (75%)
  starting transfers between devices  46.4 us (9%)
  blocking collectives  38.5 us (7%)
  between operations  14.1 us (3%)
  matrix products  13.5 us (3%)
  local copies, waits for them, and re-layouts  9.18 us (2%)
  other arithmetic  5.36 us (1%)
    psum x3, waiting for transfers between devices, local(): grad_params = lax.psum(lax.psum(lax.psum(params_part, 'z'), 'y'), 'x_lo')  238 us
    psum x1, waiting for transfers between devices, local(): lax.psum(jnp.einsum('kf,sirk->fsir', down_slice, hidden, preferred_elemen...  52.6 us
    psum x1, waiting for transfers between devices, local(): lax.psum(dispatch_part.astype(jnp.bfloat16), HALF).astype(jnp.float32)  48.2 us
    all_to_all x1, starting transfers between devices, local(): lax.all_to_all(grad_slot_in.astype(jnp.bfloat16), EXPERT, split_axis=3, c...  16.6 us
    all_to_all x1, starting transfers between devices, local(): lax.all_to_all(slot_in, EXPERT, split_axis=3, concat_axis=3, tiled=True)  16.3 us
    all_gather x1, blocking collectives, local(): logits = jnp.sum(lax.all_gather(partial_logits, axis_name=HALF), 0)  15.6 us
    all_to_all x1, waiting for transfers between devices, local(): lax.all_to_all(slot_in, EXPERT, split_axis=3, concat_axis=3, tiled=True)  15 us
    all_to_all x1, waiting for transfers between devices, local(): lax.all_to_all(grad_slot_in.astype(jnp.bfloat16), EXPERT, split_axis=3, c...  15 us
  transfers between devices with their start and end apart: 9, of which 9 were waited for; matrix products, arithmetic and copies ran while one was open for 1% of the time, Pallas kernels for 0%

profile of v1, /device:TPU:1, one launch (start us, length us, event | category | flops | bytes accessed | tf_op | source)
XLA Modules:
  0.0 514.9 jit_solution(17306503490912330313)
XLA Ops:
  7.2 1.3 convolution_bitcast_fusion.3
  8.5 15.6 %all-gather.1 = f32[4,196,256]{2,1,0:T(8,128)S(1)} all-gather(f32[1,196,256]{2,1,0:T(8,128)S(1)} %convolution_bitcast_fusion.3), channel_id=2, replica_groups=mesh['y'=4,'x_lo'=2,'z'=16,'x_hi'=2,'core'=2] {'x_hi','core'}, dimensions={0}, use_global_device_ids=true | all-gather | bytes 1003520 | tf_op jit(solution)/shard_map/all_gather | solution.py:34
  25.9 0.8 copy.45
  26.7 16.3 %all-to-all-start = ((bf16[2,1,256,128]{2,0,1,3:T(2,128)(2,1)}), bf16[2,1,256,128]{2,0,1,3:T(2,128)(2,1)S(1)}, u32[]{:S(2)}, u32[]{:S(2)}) async-start(bf16[2,1,256,128]{2,0,1,3:T(2,128)(2,1)} %copy.45), calls=%async_computation | async-start | bytes 262144 | tf_op jit(solution)/shard_map/all_to_all | solution.py:42
  44.7 15.0 %all-to-all-done = bf16[2,1,256,128]{2,0,1,3:T(2,128)(2,1)S(1)} async-done(((bf16[2,1,256,128]{2,0,1,3:T(2,128)(2,1)}), bf16[2,1,256,128]{2,0,1,3:T(2,128)(2,1)S(1)}, u32[]{:S(2)}, u32[]{:S(2)}) %all-to-all-start) | async-done | bytes 131104 | tf_op jit(solution)/shard_map/all_to_all | solution.py:42
  59.7 6.6 %all-to-all-start.2 = ((bf16[2,1,256,128]{2,0,1,3:T(2,128)(2,1)}), bf16[2,1,256,128]{2,0,1,3:T(2,128)(2,1)S(1)}, u32[]{:S(2)}, u32[]{:S(2)}) async-start(bf16[2,1,256,128]{2,0,1,3:T(2,128)(2,1)} %copy.51), calls=%async_computation.2 | async-start | bytes 262144 | tf_op jit(solution)/shard_map/all_to_all | solution.py:74
  66.4 10.7 %all_gather.14 = bf16[2,1,1024,128]{2,3,0,1:T(8,128)(2,1)S(1)} all-gather(bf16[2,1,256,128]{2,3,0,1:T(8,128)(2,1)S(1)} %copy.46), channel_id=1, replica_groups=mesh['y'=4,'x_lo'=2,'z'=16,'x_hi'=2,'core'=2] {'x_hi','core'}, dimensions={2}, use_global_device_ids=true | all-gather | bytes 655360 | tf_op jit(solution)/shard_map/all_gather | solution.py:46
  77.0 4.8 all-to-all-done.2
  81.9 12.3 %all_gather.15 = bf16[2,1,1024,128]{2,3,0,1:T(8,128)(2,1)} all-gather(bf16[2,1,256,128]{2,3,0,1:T(8,128)(2,1)S(1)} %copy.52), channel_id=1, replica_groups=mesh['y'=4,'x_lo'=2,'z'=16,'x_hi'=2,'core'=2] {'x_hi','core'}, dimensions={2}, use_global_device_ids=true | all-gather | bytes 655360 | tf_op jit(solution)/shard_map/all_gather | solution.py:78
  94.1 2.3 fusion.6
  96.4 1.0 copy-done.2
  97.4 1.6 fusion.14
  99.1 4.5 fusion.17
  103.6 52.6 %all-reduce.16.cloned.1.call-done = (bf16[1024,2,1,128]{0,3,1,2:T(8,128)(2,1)}, bf16[1024,2,1,128]{0,3,1,2:T(8,128)(2,1)}) async-done(((bf16[1024,2,1,128]{0,3,1,2:T(8,128)(2,1)}, bf16[1024,2,1,128]{0,3,1,2:T(8,128)(2,1)}), (bf16[1024,2,1,128]{0,3,1,2:T(8,128)(2,1)}, bf16[1024,2,1,128]{0,3,1,2:T(8,128)(2,1)})) %all-reduce.16.cloned.1.call-update) | async-done | bytes 1048592 | tf_op jit(solution)/shard_map/psum | solution.py:52
  156.2 0.9 convert_convert_fusion
  157.1 0.8 copy.53
  157.9 16.6 %all-to-all-start.3 = ((bf16[256,2,1,128]{0,1,2,3:T(2,128)(2,1)}), bf16[256,2,1,128]{0,1,2,3:T(2,128)(2,1)S(1)}, u32[]{:S(2)}, u32[]{:S(2)}) async-start(bf16[256,2,1,128]{0,1,2,3:T(2,128)(2,1)} %copy.53), calls=%async_computation.3 | async-start | bytes 262144 | tf_op jit(solution)/shard_map/all_to_all | solution.py:93
  174.5 0.9 convert_convert_fusion.1
  175.4 0.8 copy.47
  176.2 15.0 %all-to-all-done.3 = bf16[256,2,1,128]{0,1,2,3:T(2,128)(2,1)S(1)} async-done(((bf16[256,2,1,128]{0,1,2,3:T(2,128)(2,1)}), bf16[256,2,1,128]{0,1,2,3:T(2,128)(2,1)S(1)}, u32[]{:S(2)}, u32[]{:S(2)}) %all-to-all-start.3) | async-done | bytes 131104 | tf_op jit(solution)/shard_map/all_to_all | solution.py:93
  191.2 6.6 %all-to-all-start.1 = ((bf16[256,2,1,128]{0,1,2,3:T(2,128)(2,1)}), bf16[256,2,1,128]{0,1,2,3:T(2,128)(2,1)S(1)}, u32[]{:S(2)}, u32[]{:S(2)}) async-start(bf16[256,2,1,128]{0,1,2,3:T(2,128)(2,1)} %copy.47), calls=%async_computation.1 | async-start | bytes 262144 | tf_op jit(solution)/shard_map/all_to_all | solution.py:61
  199.3 14.1 %all-to-all-done.1 = bf16[256,2,1,128]{0,1,2,3:T(2,128)(2,1)S(1)} async-done(((bf16[256,2,1,128]{0,1,2,3:T(2,128)(2,1)}), bf16[256,2,1,128]{0,1,2,3:T(2,128)(2,1)S(1)}, u32[]{:S(2)}, u32[]{:S(2)}) %all-to-all-start.1) | async-done | bytes 131104 | tf_op jit(solution)/shard_map/all_to_all | solution.py:61
  214.8 48.2 %all-reduce.14.cloned.1.call-done = (bf16[1,196,256]{2,1,0:T(8,128)(2,1)}, bf16[1,196,256]{2,1,0:T(8,128)(2,1)}) async-done(((bf16[1,196,256]{2,1,0:T(8,128)(2,1)}, bf16[1,196,256]{2,1,0:T(8,128)(2,1)}), (bf16[1,196,256]{2,1,0:T(8,128)(2,1)}, bf16[1,196,256]{2,1,0:T(8,128)(2,1)})) %all-reduce.14.cloned.1.call-update) | async-done | bytes 200720 | tf_op jit(solution)/shard_map/psum | solution.py:99
  263.0 1.2 fusion.52
  264.2 1.1 fusion.67
  265.3 0.9 convolution_bitcast_fusion
  266.3 126.5 %all-reduce.8.cloned.1.call-done = f32[256,256]{0,1:T(8,128)} async-done(((f32[256,256]{0,1:T(8,128)}), f32[256,256]{0,1:T(8,128)}) %all-reduce.8.cloned.1.call-update) | async-done | bytes 262160 | tf_op jit(solution)/shard_map/psum | solution.py:112
  392.9 0.9 fusion.20
  393.8 62.7 %all-reduce.10.cloned.1.call-done = f32[256,256]{0,1:T(8,128)} async-done(((f32[256,256]{0,1:T(8,128)}), f32[256,256]{0,1:T(8,128)}) %all-reduce.10.cloned.1.call-update) | async-done | bytes 262160 | tf_op jit(solution)/shard_map/psum | solution.py:112
  456.7 0.9 fusion.21
  457.6 49.1 %all-reduce.12.cloned.1.call-done = f32[256,256]{0,1:T(8,128)} async-done(((f32[256,256]{0,1:T(8,128)}), f32[256,256]{0,1:T(8,128)}) %all-reduce.12.cloned.1.call-update) | async-done | bytes 262160 | tf_op jit(solution)/shard_map/psum | solution.py:112
  506.6 1.8 copy.60
  (49 shorter events, 6.6 us)
Async XLA Ops:
  7.2 90.3 %copy-start = (bf16[1,1024,1024]{2,1,0:T(8,128)(2,1)S(1)}, bf16[1,1024,1024]{2,1,0:T(8,128)(2,1)}, u32[]{:S(2)}) copy-start(bf16[1,1024,1024]{2,1,0:T(8,128)(2,1)} %param.8) | copy-start | bytes 6291460
  8.5 17.2 %copy-start.1 = (bf16[196,256]{1,0:T(8,128)(2,1)S(1)}, bf16[196,256]{1,0:T(8,128)(2,1)}, u32[]{:S(2)}) copy-start(bf16[196,256]{1,0:T(8,128)(2,1)} %param.5) | copy-start | bytes 301060
  24.2 19.5 %copy-start.5 = (bf16[196,256]{1,0:T(8,128)(2,1)S(1)}, bf16[196,256]{1,0:T(8,128)(2,1)}, u32[]{:S(2)}) copy-start(bf16[196,256]{1,0:T(8,128)(2,1)} %param.9) | copy-start | bytes 301060
  26.7 33.0 %all-to-all-start = ((bf16[2,1,256,128]{2,0,1,3:T(2,128)(2,1)}), bf16[2,1,256,128]{2,0,1,3:T(2,128)(2,1)S(1)}, u32[]{:S(2)}, u32[]{:S(2)}) async-start(bf16[2,1,256,128]{2,0,1,3:T(2,128)(2,1)} %copy.45), calls=%async_computation | async-start | bytes 262144 | tf_op jit(solution)/shard_map/all_to_all | solution.py:42
  59.7 22.2 %all-to-all-start.2 = ((bf16[2,1,256,128]{2,0,1,3:T(2,128)(2,1)}), bf16[2,1,256,128]{2,0,1,3:T(2,128)(2,1)S(1)}, u32[]{:S(2)}, u32[]{:S(2)}) async-start(bf16[2,1,256,128]{2,0,1,3:T(2,128)(2,1)} %copy.51), calls=%async_computation.2 | async-start | bytes 262144 | tf_op jit(solution)/shard_map/all_to_all | solution.py:74
  66.3 89.9 %all-reduce.16.cloned.1.call-start = ((), (), s32[]{:S(2)}) async-start(), calls=%async_computation.8 | async-start | bytes 2097152 | tf_op jit(solution)/shard_map/psum | solution.py:52
  96.4 1.0 copy-start.2
  97.4 1.6 copy-start.3
  157.9 33.3 %all-to-all-start.3 = ((bf16[256,2,1,128]{0,1,2,3:T(2,128)(2,1)}), bf16[256,2,1,128]{0,1,2,3:T(2,128)(2,1)S(1)}, u32[]{:S(2)}, u32[]{:S(2)}) async-start(bf16[256,2,1,128]{0,1,2,3:T(2,128)(2,1)} %copy.53), calls=%async_computation.3 | async-start | bytes 262144 | tf_op jit(solution)/shard_map/all_to_all | solution.py:93
  191.2 22.1 %all-to-all-start.1 = ((bf16[256,2,1,128]{0,1,2,3:T(2,128)(2,1)}), bf16[256,2,1,128]{0,1,2,3:T(2,128)(2,1)S(1)}, u32[]{:S(2)}, u32[]{:S(2)}) async-start(bf16[256,2,1,128]{0,1,2,3:T(2,128)(2,1)} %copy.47), calls=%async_computation.1 | async-start | bytes 262144 | tf_op jit(solution)/shard_map/all_to_all | solution.py:61
  197.8 65.2 %all-reduce.14.cloned.1.call-start = ((), (), s32[]{:S(2)}) async-start(), calls=%async_computation.7 | async-start | bytes 409600 | tf_op jit(solution)/shard_map/psum | solution.py:99
  213.5 243.2 %copy-start.4 = (bf16[256,256]{1,0:T(8,128)(2,1)S(1)}, bf16[256,256]{1,0:T(8,128)(2,1)}, u32[]{:S(2)}) copy-start(bf16[256,256]{1,0:T(8,128)(2,1)} %param.6) | copy-start | bytes 393220
  214.8 178.0 %all-reduce.8.cloned.1.call-start = ((), (), s32[]{:S(2)}) async-start(), calls=%async_computation.4 | async-start | bytes 524288 | tf_op jit(solution)/shard_map/psum | solution.py:112
  266.3 190.2 %all-reduce.10.cloned.1.call-start = ((), (), s32[]{:S(2)}) async-start(), calls=%async_computation.5 | async-start | bytes 524288 | tf_op jit(solution)/shard_map/psum | solution.py:112
  392.8 113.8 %all-reduce.12.cloned.1.call-start = ((), (), s32[]{:S(2)}) async-start(), calls=%async_computation.6 | async-start | bytes 524288 | tf_op jit(solution)/shard_map/psum | solution.py:112
Sparse Core Ops, SparseCore 0:
  103.7 52.4 all-reduce.15
  214.9 48.0 all-reduce.13
  266.4 126.3 all-reduce.7
  395.0 61.3 all-reduce.9
  459.1 47.4 all-reduce.11
